TPU v7x, 128 devices: a whole 4x4x4 slice. The times are simulated.
128 devices in a mesh: chan: 8 (over z, core), sec: 16 (over y, x).
Axes of the slice: x: 4, y: 4, z: 4, core: 2. Of those that a mesh axis runs over, the one named last changes fastest.
Arguments:
- psi: bfloat16 [384, 4, 256, 256], P('sec'), may hold values from -6 to 6
- mpo: float32 [8, 4, 4], P('chan'), may hold values from -1 to 1
- left_env: bfloat16 [8, 128, 256, 256], P('chan', 'sec'), may hold values from -0.375 to 0.375
- right_env: bfloat16 [8, 384, 256, 256], P('chan', 'sec'), may hold values from -0.375 to 0.375
- left_dims: int32 [128], P('sec'), may hold values from 128 to 256, as said below
- right_dims: int32 [384], P('sec'), may hold values from 128 to 256, as said below
- dest_owner: int32 [384, 1], P('sec'), may hold values from 0 to 15, as said below
- left_slot: int32 [384], P('sec'), may hold values from 0 to 7
Outputs:
- h_psi: bfloat16 [384, 4, 256, 256], P('sec', None, 'chan')
Inputs may be any that keep to these rules, and one draw needn't show every extreme that they name: `dest_owner`: each device's 24 blocks name one owner at most 2 times; in every draw some owner is named exactly 2 times by the blocks of every device. `left_dims`: multiples of 128; both bounds are reached. `right_dims`: multiples of 128; both bounds are reached.
All inputs are finite; a program needn't handle non-finite values.
Results may differ from a plain program's by a relative error of at most 0.014.
Values may be sent and summed in bfloat16 or wider, within the bound.
A program may use at most 192 MiB of HBM per device.

v0:
```python
import jax
import jax.numpy as jnp
from jax import lax
from jax.sharding import PartitionSpec as P


def on_device(psi, mpo, left_env, right_env, left_dims, right_dims, dest_owner, left_slot):
    block_width = psi.shape[2]
    blocks = psi.shape[0]
    sectors = left_env.shape[1]
    owners = lax.axis_size("sec")
    capacity = max(2, (blocks + owners - 1) // owners)
    places = jnp.arange(block_width, dtype=jnp.int32)
    right_mask = (places[None, :] < right_dims[:, None]).astype(jnp.bfloat16)
    left_mask = (places[None, :] < left_dims[:, None]).astype(jnp.bfloat16)
    right_kept = right_env[0] * (right_mask[:, :, None] * right_mask[:, None, :])
    left_kept = left_env[0] * (left_mask[:, :, None] * left_mask[:, None, :])
    inner = jnp.einsum("kpac,kdc->kpad", psi, right_kept, preferred_element_type=jnp.float32)
    mixed = jnp.einsum("sp,kpad->ksad", mpo[0], inner, precision=lax.Precision.HIGHEST).astype(
        jnp.bfloat16
    )
    target = dest_owner[:, 0]
    marks = (target[:, None] == jnp.arange(owners, dtype=jnp.int32)[None, :]).astype(jnp.int32)
    position = jnp.sum(jnp.cumsum(marks, axis=0) * marks, axis=1) - 1
    slot_of = target * capacity + position
    filled = (
        jnp.zeros((owners * capacity,), jnp.int32)
        .at[slot_of]
        .set(jnp.arange(blocks, dtype=jnp.int32) + 1)
    )
    source = jnp.where(filled > 0, filled - 1, blocks)
    outbound = jnp.take(mixed, source, axis=0, mode="fill", fill_value=0)
    outbound = outbound.reshape((owners, capacity) + mixed.shape[1:])
    slot_ids = jnp.where(filled > 0, jnp.take(left_slot, jnp.clip(source, 0, blocks - 1)), sectors)
    slot_ids = slot_ids.reshape(owners, capacity)
    arrived = lax.all_to_all(outbound, "sec", split_axis=0, concat_axis=0, tiled=True)
    sector_ids = lax.all_to_all(slot_ids, "sec", split_axis=0, concat_axis=0, tiled=True)
    picked = jnp.take(left_kept, sector_ids, axis=0, mode="fill", fill_value=0)
    product = jnp.einsum("nkea,nksad->nksed", picked, arrived, preferred_element_type=jnp.float32)
    reduced = lax.psum_scatter(
        product.astype(jnp.bfloat16), "chan", scatter_dimension=3, tiled=True
    )
    returned = lax.all_to_all(reduced, "sec", split_axis=0, concat_axis=0, tiled=True)
    flattened = returned.reshape((owners * capacity,) + returned.shape[2:])
    own_rows = jnp.take(flattened, slot_of, axis=0)
    return own_rows


def solution(mesh):
    in_specs = (
        P("sec", None, None, None),
        P("chan", None, None),
        P("chan", "sec", None, None),
        P("chan", "sec", None, None),
        P("sec"),
        P("sec"),
        P("sec", None),
        P("sec"),
    )
    out_specs = P("sec", None, "chan", None)
    return jax.shard_map(
        on_device, mesh=mesh, in_specs=in_specs, out_specs=out_specs, check_vma=False
    )
```

profile of v0, /device:TPU:0, one launch (start us, length us, event | category | flops | bytes accessed | tf_op | source)
XLA Modules:
  0.0 610.1 jit_solution(2105625664643277036)
XLA Ops:
  6.5 0.0 copy-start
  6.5 0.7 fusion.9
  7.3 0.8 select_reduce_fusion
  8.2 0.7 and_bitcast_fusion
  8.8 0.6 scatter_custom_fusion
  9.5 1.4 gather_fusion.1
  10.9 0.7 all_to_all.17
  11.6 7.1 %all-to-all-start.1 = ((s32[16,1,2]{2,1,0:T(1,128)}), s32[16,1,2]{2,1,0:T(1,128)S(1)}, u32[]{:S(2)}, u32[]{:S(2)}) async-start(s32[16,1,2]{2,1,0:T(1,128)} %bitcast.13), calls=%async_computation.1 | async-start | bytes 16384 | tf_op jit(solution)/shard_map/all_to_all | solution.py:37
  18.7 0.7 fusion.8
  19.5 13.3 %convolution_bitcast_fusion = f32[24,4,256,256]{2,3,1,0:T(8,128)} fusion(bf16[24,4,256,256]{3,2,1,0:T(8,128)(2,1)} %param.8, bf16[1,24,256,256]{3,2,1,0:T(8,128)(2,1)} %param.11, bf16[24,256]{1,0:T(8,128)(2,1)S(1)} %fusion.8), kind=kOutput, calls=%fused_computation.8 | convolution fusion | flops 3230662656 | bytes 40906752 | tf_op jit(solution)/shard_map/kpac,kdc->kpad/dot_general | solution.py:18
  32.8 28.5 %copy.20 = f32[24,4,256,256]{3,1,2,0:T(4,128)} copy(f32[24,4,256,256]{2,3,1,0:T(8,128)} %convolution_bitcast_fusion) | data formatting | bytes 50331648 | tf_op jit(solution)/shard_map/kpac,kdc->kpad/dot_general | solution.py:18
  61.3 0.0 copy-done
  61.3 47.5 %convert_bitcast_fusion.1 = bf16[24,4,256,256]{3,1,2,0:T(4,128)(2,1)} fusion(f32[24,4,256,256]{3,1,2,0:T(4,128)} %copy.20, f32[1,4,4]{2,1,0:T(4,128)S(1)} %copy-done), kind=kOutput, calls=%fused_computation.7 | convolution fusion | flops 308281344 | bytes 37748800 | tf_op jit(solution)/shard_map/sp,kpad->ksad/dot_general | solution.py:19
  108.8 20.7 %gather_fusion = bf16[32,4,256,256]{3,1,2,0:T(4,128)(2,1)} fusion(bf16[24,4,256,256]{3,1,2,0:T(4,128)(2,1)} %convert_bitcast_fusion.1, s32[1024]{0:T(1024)S(1)} %pad_clamp_fusion.3), kind=kCustom, calls=%fused_computation | custom fusion | bytes 33554560 | tf_op jit(solution)/shard_map/jit(_take)/gather | solution.py:32
  129.5 26.2 %copy.21 = bf16[16,2,4,256,256]{3,4,2,1,0:T(8,128)(2,1)} copy(bf16[16,2,4,256,256]{4,2,3,1,0:T(4,128)(2,1)} %bitcast.52) | data formatting | bytes 33554432 | tf_op jit(solution)/shard_map/jit(_take)/gather | solution.py:32
  155.7 0.1 broadcast_in_dim.61
  155.8 14.0 %broadcast_select_fusion = bf16[16,2,4,256,256]{3,4,2,1,0:T(8,128)(2,1)} fusion(bf16[16,2,4,256,256]{3,4,2,1,0:T(8,128)(2,1)} %copy.21, pred[16,2]{1,0:T(8,128)(4,1)S(1)} %broadcast_in_dim.61), kind=kLoop, calls=%fused_computation.6 | loop fusion | flops 8388608 | bytes 33554464 | tf_op jit(solution)/shard_map/jit(_take)/select_n | solution.py:32
  169.8 0.0 copy-start.3
  169.8 0.0 copy-start.2
  169.8 0.0 all-to-all-done.1
  169.8 7.5 %all-to-all-start = ((bf16[16,2,4,256,256]{3,4,2,1,0:T(8,128)(2,1)}), bf16[16,2,4,256,256]{3,4,2,1,0:T(8,128)(2,1)}, u32[]{:S(2)}, u32[]{:S(2)}) async-start(bf16[16,2,4,256,256]{3,4,2,1,0:T(8,128)(2,1)} %broadcast_select_fusion), calls=%async_computation | async-start | bytes 33554432 | tf_op jit(solution)/shard_map/all_to_all | solution.py:36
  177.3 0.0 reduce-scatter.2.cloned.1.call-start
  177.3 0.0 copy-done.3
  177.3 0.1 fusion.10
  177.4 0.0 copy-done.2
  177.4 0.3 bitcast_multiply_fusion.2
  177.8 0.1 copy.23
  177.9 0.1 copy.26
  177.9 0.1 reshape.164
  178.0 0.1 copy.24
  178.2 2.9 gather_fusion.2
  181.0 243.2 %all-to-all-done = bf16[16,2,4,256,256]{3,4,2,1,0:T(8,128)(2,1)} async-done(((bf16[16,2,4,256,256]{3,4,2,1,0:T(8,128)(2,1)}), bf16[16,2,4,256,256]{3,4,2,1,0:T(8,128)(2,1)}, u32[]{:S(2)}, u32[]{:S(2)}) %all-to-all-start) | async-done | bytes 16777248 | tf_op jit(solution)/shard_map/all_to_all | solution.py:36
  424.2 12.6 %convert_bitcast_fusion = bf16[16,2,4,256,256]{3,4,2,1,0:T(8,128)(2,1)} fusion(bf16[16,2,4,256,256]{3,4,2,1,0:T(8,128)(2,1)} %all-to-all-done, bf16[16,2,256,256]{3,2,1,0:T(8,128)(2,1)} %bitcast.53, pred[16,2]{1,0:T(8,128)(4,1)S(1)} %copy.24), kind=kOutput, calls=%fused_computation.5 | convolution fusion | flops 4305453056 | bytes 37748768 | tf_op jit(solution)/shard_map/nkea,nksad->nksed/dot_general | solution.py:39
  436.9 28.1 %copy.27 = bf16[16,2,4,256,256]{4,0,2,1,3:T(8,128)(2,1)} copy(bf16[16,2,4,256,256]{3,4,2,1,0:T(8,128)(2,1)} %convert_bitcast_fusion) | data formatting | bytes 33554432 | tf_op jit(solution)/shard_map/convert_element_type | solution.py:41
  464.9 0.0 reduce-scatter.2.cloned.1.call-update
  465.0 92.6 %reduce-scatter.2.cloned.1.call-done = bf16[16,2,4,32,256]{4,0,2,1,3:T(8,128)(2,1)} async-done(((bf16[16,2,4,256,256]{4,0,2,1,3:T(8,128)(2,1)}), bf16[16,2,4,32,256]{4,0,2,1,3:T(8,128)(2,1)}) %reduce-scatter.2.cloned.1.call-update) | async-done | bytes 2097168 | tf_op jit(solution)/shard_map/reduce_scatter | solution.py:40
  557.6 0.0 copy-start.1
  557.6 4.1 copy.28
  561.7 6.8 %all-to-all-start.2 = ((bf16[16,2,4,32,256]{4,3,2,1,0:T(8,128)(2,1)}), bf16[16,2,4,32,256]{4,3,2,1,0:T(8,128)(2,1)S(1)}, u32[]{:S(2)}, u32[]{:S(2)}) async-start(bf16[16,2,4,32,256]{4,3,2,1,0:T(8,128)(2,1)} %copy.28), calls=%async_computation.3 | async-start | bytes 4194304 | tf_op jit(solution)/shard_map/all_to_all | solution.py:43
  568.5 30.2 %all-to-all-done.2 = bf16[16,2,4,32,256]{4,3,2,1,0:T(8,128)(2,1)S(1)} async-done(((bf16[16,2,4,32,256]{4,3,2,1,0:T(8,128)(2,1)}), bf16[16,2,4,32,256]{4,3,2,1,0:T(8,128)(2,1)S(1)}, u32[]{:S(2)}, u32[]{:S(2)}) %all-to-all-start.2) | async-done | bytes 2097184 | tf_op jit(solution)/shard_map/all_to_all | solution.py:43
  598.7 1.8 gather_fusion.3
  600.5 2.8 broadcast_select_fusion.1
  603.3 0.0 copy-done.1
  (11 shorter events, 0.1 us)
Async XLA Ops:
  6.5 54.8 %copy-start = (f32[1,4,4]{2,1,0:T(4,128)S(1)}, f32[1,4,4]{2,1,0:T(4,128)}, u32[]{:S(2)}) copy-start(f32[1,4,4]{2,1,0:T(4,128)} %param.9) | copy-start | bytes 196
  11.6 158.2 %all-to-all-start.1 = ((s32[16,1,2]{2,1,0:T(1,128)}), s32[16,1,2]{2,1,0:T(1,128)S(1)}, u32[]{:S(2)}, u32[]{:S(2)}) async-start(s32[16,1,2]{2,1,0:T(1,128)} %bitcast.13), calls=%async_computation.1 | async-start | bytes 16384 | tf_op jit(solution)/shard_map/all_to_all | solution.py:37
  169.8 7.5 %copy-start.3 = (s32[8]{0:T(128)S(1)}, s32[8]{0:T(128)}, u32[]{:S(2)}) copy-start(s32[8]{0:T(128)} %param.12) | copy-start | bytes 100
  169.8 7.6 %copy-start.2 = (bf16[1,8,256,256]{3,2,1,0:T(8,128)(2,1)S(1)}, bf16[1,8,256,256]{3,2,1,0:T(8,128)(2,1)}, u32[]{:S(2)}) copy-start(bf16[1,8,256,256]{3,2,1,0:T(8,128)(2,1)} %param.10) | copy-start | bytes 3145732
  169.8 254.4 %all-to-all-start = ((bf16[16,2,4,256,256]{3,4,2,1,0:T(8,128)(2,1)}), bf16[16,2,4,256,256]{3,4,2,1,0:T(8,128)(2,1)}, u32[]{:S(2)}, u32[]{:S(2)}) async-start(bf16[16,2,4,256,256]{3,4,2,1,0:T(8,128)(2,1)} %broadcast_select_fusion), calls=%async_computation | async-start | bytes 33554432 | tf_op jit(solution)/shard_map/all_to_all | solution.py:36
  177.3 380.3 %reduce-scatter.2.cloned.1.call-start = ((), (), s32[]{:S(2)}) async-start(), calls=%async_computation.4 | async-start | bytes 18874368 | tf_op jit(solution)/shard_map/reduce_scatter | solution.py:40
  557.6 45.7 %copy-start.1 = (f32[1,4,4]{2,1,0:T(4,128)S(1)}, f32[1,4,4]{2,1,0:T(4,128)}, u32[]{:S(2)}) copy-start(f32[1,4,4]{2,1,0:T(4,128)} %param.9) | copy-start | bytes 196
  561.7 37.0 %all-to-all-start.2 = ((bf16[16,2,4,32,256]{4,3,2,1,0:T(8,128)(2,1)}), bf16[16,2,4,32,256]{4,3,2,1,0:T(8,128)(2,1)S(1)}, u32[]{:S(2)}, u32[]{:S(2)}) async-start(bf16[16,2,4,32,256]{4,3,2,1,0:T(8,128)(2,1)} %copy.28), calls=%async_computation.3 | async-start | bytes 4194304 | tf_op jit(solution)/shard_map/all_to_all | solution.py:43
Sparse Core Ops, SparseCore 0:
  465.1 92.4 reduce-scatter.1
where the time goes:
time: 615 us; the launch traced here: 610 us
  waiting for transfers between devices  366 us (60%)
  local copies, waits for them, and re-layouts  115 us (19%)
  matrix products  73.5 us (12%)
  starting transfers between devices  21.5 us (3%)
  other arithmetic  20.2 us (3%)
  between operations  13.5 us (2%)
    all_to_all x1, waiting for transfers between devices, on_device(): lax.all_to_all(outbound, 'sec', split_axis=0, concat_axis=0, tiled=True)  243 us
    reduce_scatter x1, waiting for transfers between devices, on_device(): lax.psum_scatter(product.astype(jnp.bfloat16), 'chan', scatter_dimension=...  92.6 us
    dot_general x1, matrix products, on_device(): jnp.einsum('sp,kpad->ksad', mpo[0], inner, precision=lax.Precision.HIGHEST)  47.5 us
    gather x2, local copies, waits for them, and re-layouts, on_device(): outbound = jnp.take(mixed, source, axis=0, mode='fill', fill_value=0)  46.9 us
    all_to_all x1, waiting for transfers between devices, on_device(): lax.all_to_all(reduced, 'sec', split_axis=0, concat_axis=0, tiled=True)  30.2 us
    dot_general x1, local copies, waits for them, and re-layouts, on_device(): jnp.einsum('kpac,kdc->kpad', psi, right_kept, preferred_element_type=jnp....  28.5 us
    convert_element_type x1, local copies, waits for them, and re-layouts, on_device(): product.astype(jnp.bfloat16)  28.1 us
    select_n x1, other arithmetic, on_device(): outbound = jnp.take(mixed, source, axis=0, mode='fill', fill_value=0)  14 us
  transfers between devices with their start and end apart: 4, of which 3 were waited for; matrix products, arithmetic and copies ran while one was open for 25% of the time, Pallas kernels for 0%

commit v1 on v0

v1 whole, which is shorter than its diff:
```python
import jax
import jax.numpy as jnp
from jax import lax
from jax.sharding import PartitionSpec as P


def on_device(psi, mpo, left_env, right_env, left_dims, right_dims, dest_owner, left_slot):
    block_width = psi.shape[2]
    blocks = psi.shape[0]
    owners = lax.axis_size("sec")
    capacity = max(2, (blocks + owners - 1) // owners)
    places = jnp.arange(block_width, dtype=jnp.int32)
    right_mask = (places[None, :] < right_dims[:, None]).astype(jnp.bfloat16)
    left_mask = (places[None, :] < left_dims[:, None]).astype(jnp.bfloat16)
    target = dest_owner[:, 0]
    marks = (target[:, None] == jnp.arange(owners, dtype=jnp.int32)[None, :]).astype(jnp.int32)
    position = jnp.sum(jnp.cumsum(marks, axis=0) * marks, axis=1) - 1
    slot_of = target * capacity + position
    here = slot_of[:, None] == jnp.arange(owners * capacity, dtype=jnp.int32)[None, :]
    wanted = jnp.sum(jnp.where(here, left_slot[:, None], 0), axis=0)
    asked = lax.all_to_all(
        wanted.reshape(owners, capacity), "sec", split_axis=0, concat_axis=0, tiled=True
    )
    left_kept = left_env[0] * (left_mask[:, :, None] * left_mask[:, None, :])
    outbound = jnp.take(left_kept, asked, axis=0, mode="clip")
    arrived = lax.all_to_all(outbound, "sec", split_axis=0, concat_axis=0, tiled=True)
    right_kept = right_env[0] * (right_mask[:, :, None] * right_mask[:, None, :])
    inner = jnp.einsum("kpac,kdc->kpad", psi, right_kept, preferred_element_type=jnp.float32)
    mixed = jnp.einsum("sp,kpad->ksad", mpo[0], inner, precision=lax.Precision.HIGHEST).astype(
        jnp.bfloat16
    )
    picked = jnp.take(
        arrived.reshape((owners * capacity,) + arrived.shape[2:]), slot_of, axis=0, mode="clip"
    )
    product = jnp.einsum("kea,ksad->ksed", picked, mixed, preferred_element_type=jnp.float32)
    return lax.psum_scatter(
        product.astype(jnp.bfloat16), "chan", scatter_dimension=2, tiled=True
    )


def solution(mesh):
    in_specs = (
        P("sec", None, None, None),
        P("chan", None, None),
        P("chan", "sec", None, None),
        P("chan", "sec", None, None),
        P("sec"),
        P("sec"),
        P("sec", None),
        P("sec"),
    )
    out_specs = P("sec", None, "chan", None)
    return jax.shard_map(
        on_device, mesh=mesh, in_specs=in_specs, out_specs=out_specs, check_vma=False
    )
```

time: 615 us -> 229 us (0.37)
  waiting for transfers between devices: 366 us -> 79.7 us
  local copies, waits for them, and re-layouts: 115 us -> 26.9 us
  matrix products: 73.5 us -> 89.1 us
  other arithmetic: 20.2 us -> 6.73 us
  starting transfers between devices: 21.5 us -> 12 us
    all_to_all x1, waiting for transfers between devices: 243 us -> 0.01 us  [on_device(): lax.all_to_all(outbound, 'sec', split_axis=0, concat_axis=0, tiled=True)]
    gather x5 -> x2, local copies, waits for them, and re-layouts: 53 us -> 5.66 us  [the longest x1 2.94 us: on_device(): jnp.take(arrived.reshape((owners * capacity,) + arrived.shape[2:]), slot_...]
    dot_general x1 -> x0, local copies, waits for them, and re-layouts: 28.5 us -> none  [on_device(): jnp.einsum('kpac,kdc->kpad', psi, right_kept, preferred_element_type=jnp....]
    all_to_all x2 -> x1, waiting for transfers between devices: 30.2 us -> 4.48 us  [on_device(): lax.all_to_all(wanted.reshape(owners, capacity), 'sec', split_axis=0, con...]
    dot_general x1, matrix products: 47.5 us -> 65.4 us  [on_device(): jnp.einsum('sp,kpad->ksad', mpo[0], inner, precision=lax.Precision.HIGHEST)]
    reduce_scatter x1, waiting for transfers between devices: 92.6 us -> 75.2 us  [on_device(): lax.psum_scatter(product.astype(jnp.bfloat16), 'chan', scatter_dimension=...]
    select_n x5 -> x0, other arithmetic: 16.8 us -> none  [the longest x1 14 us: on_device(): outbound = jnp.take(mixed, source, axis=0, mode='fill', fill_value=0)]
    convert_element_type x1, local copies, waits for them, and re-layouts: 28.1 us -> 16.5 us  [on_device(): product.astype(jnp.bfloat16)]
  transfers between devices with their start and end apart: 4 -> 3, of which waited for: 3 -> 2; matrix products, arithmetic and copies ran while one was open for 25% -> 36% of each run, Pallas kernels for 0% -> 0%
where the time goes in v1:
time: 229 us; the launch traced here: 228 us
  matrix products  89.1 us (39%)
  waiting for transfers between devices  79.7 us (35%)
  local copies, waits for them, and re-layouts  26.9 us (12%)
  between operations  13.5 us (6%)
  starting transfers between devices  12 us (5%)
  other arithmetic  6.73 us (3%)
    reduce_scatter x1, waiting for transfers between devices, on_device(): lax.psum_scatter(product.astype(jnp.bfloat16), 'chan', scatter_dimension=...  75.2 us
    dot_general x1, matrix products, on_device(): jnp.einsum('sp,kpad->ksad', mpo[0], inner, precision=lax.Precision.HIGHEST)  65.4 us
    convert_element_type x1, local copies, waits for them, and re-layouts, on_device(): product.astype(jnp.bfloat16)  16.5 us
    dot_general x1, matrix products, on_device(): jnp.einsum('kpac,kdc->kpad', psi, right_kept, preferred_element_type=jnp....  12.9 us
    dot_general x1, matrix products, on_device(): jnp.einsum('kea,ksad->ksed', picked, mixed, preferred_element_type=jnp.fl...  10.8 us
    all_to_all x1, starting transfers between devices, on_device(): lax.all_to_all(wanted.reshape(owners, capacity), 'sec', split_axis=0, con...  7.15 us
    all_to_all x1, starting transfers between devices, on_device(): lax.all_to_all(outbound, 'sec', split_axis=0, concat_axis=0, tiled=True)  4.81 us
  transfers between devices with their start and end apart: 3, of which 2 were waited for; matrix products, arithmetic and copies ran while one was open for 36% of the time, Pallas kernels for 0%

profile of v1, /device:TPU:0, one launch (start us, length us, event | category | flops | bytes accessed | tf_op | source)
XLA Modules:
  0.0 228.0 jit_solution(1563769119673781832)
XLA Ops:
  6.5 0.0 copy-start
  6.5 0.7 fusion.14
  7.3 0.8 select_reduce_fusion.1
  8.2 0.7 fusion.17
  8.8 0.7 select_reduce_fusion
  9.6 0.7 all_to_all.9
  10.3 7.1 %all-to-all-start = ((s32[16,1,2]{2,1,0:T(1,128)}), s32[16,1,2]{2,1,0:T(1,128)S(1)}, u32[]{:S(2)}, u32[]{:S(2)}) async-start(s32[16,1,2]{2,1,0:T(1,128)} %bitcast.12), calls=%async_computation | async-start | bytes 16384 | tf_op jit(solution)/shard_map/all_to_all | solution.py:21
  17.4 0.7 fusion.15
  18.1 1.6 bitcast_multiply_fusion.2
  19.7 0.7 fusion.13
  20.4 4.5 %all-to-all-done = s32[16,1,2]{2,1,0:T(1,128)S(1)} async-done(((s32[16,1,2]{2,1,0:T(1,128)}), s32[16,1,2]{2,1,0:T(1,128)S(1)}, u32[]{:S(2)}, u32[]{:S(2)}) %all-to-all-start) | async-done | bytes 160 | tf_op jit(solution)/shard_map/all_to_all | solution.py:21
  24.9 0.5 broadcast.84
  25.4 0.7 reduce.3
  26.1 0.1 reshape.97
  26.2 2.7 %gather_fusion = bf16[32,256,256]{2,1,0:T(8,128)(2,1)} fusion(bf16[8,256,256]{2,1,0:T(8,128)(2,1)S(1)} %bitcast_multiply_fusion.2, s32[1024]{0:T(1024)S(1)} %pad_clamp_fusion.1), kind=kCustom, calls=%fused_computation | custom fusion | bytes 8388736 | tf_op jit(solution)/shard_map/jit(_take)/gather | solution.py:25
  28.9 0.0 copy-start.2
  28.9 4.8 %all-to-all-start.1 = ((bf16[16,2,256,256]{3,2,1,0:T(8,128)(2,1)}), bf16[16,2,256,256]{3,2,1,0:T(8,128)(2,1)}, u32[]{:S(2)}, u32[]{:S(2)}) async-start(bf16[16,2,256,256]{3,2,1,0:T(8,128)(2,1)} %bitcast.41), calls=%async_computation.1 | async-start | bytes 8388608 | tf_op jit(solution)/shard_map/all_to_all | solution.py:26
  33.8 0.0 reduce-scatter.2.cloned.1.call-start
  33.8 0.0 copy-done.2
  33.8 12.9 %convolution_bitcast_fusion = f32[24,4,256,256]{2,3,1,0:T(8,128)} fusion(bf16[24,4,256,256]{3,2,1,0:T(8,128)(2,1)} %param.8, bf16[1,24,256,256]{3,2,1,0:T(8,128)(2,1)S(1)} %copy-done.2, bf16[24,256]{1,0:T(8,128)(2,1)S(1)} %fusion.13), kind=kOutput, calls=%fused_computation.8 | convolution fusion | flops 3230662656 | bytes 40906752 | tf_op jit(solution)/shard_map/kpac,kdc->kpad/dot_general | solution.py:28
  46.7 0.0 copy-done
  46.7 65.4 %convert_bitcast_fusion.1 = bf16[24,4,256,256]{2,1,3,0:T(4,128)(2,1)} fusion(f32[24,4,256,256]{2,3,1,0:T(8,128)} %convolution_bitcast_fusion, f32[1,4,4]{2,1,0:T(4,128)S(1)} %copy-done), kind=kOutput, calls=%fused_computation.7 | convolution fusion | flops 308281344 | bytes 37748800 | tf_op jit(solution)/shard_map/sp,kpad->ksad/dot_general | solution.py:29
  112.1 0.0 all-to-all-done.1
  112.1 2.9 %gather_fusion.1 = bf16[24,256,256]{2,1,0:T(8,128)(2,1)S(1)} fusion(bf16[32,256,256]{2,1,0:T(8,128)(2,1)} %bitcast.14, s32[1024]{0:T(1024)S(1)} %pad_clamp_fusion), kind=kCustom, calls=%fused_computation.1 | custom fusion | bytes 6291552 | tf_op jit(solution)/shard_map/jit(_take)/gather | solution.py:32
  115.1 10.8 %convert_bitcast_fusion = bf16[24,4,256,256]{2,3,1,0:T(8,128)(2,1)} fusion(bf16[24,4,256,256]{2,1,3,0:T(4,128)(2,1)} %convert_bitcast_fusion.1, bf16[24,256,256]{2,1,0:T(8,128)(2,1)S(1)} %gather_fusion.1), kind=kOutput, calls=%fused_computation.6 | convolution fusion | flops 3227516928 | bytes 28311552 | tf_op jit(solution)/shard_map/kea,ksad->ksed/dot_general | solution.py:35
  125.9 16.5 %copy.19 = bf16[24,4,256,256]{3,0,1,2:T(8,128)(2,1)} copy(bf16[24,4,256,256]{2,3,1,0:T(8,128)(2,1)} %convert_bitcast_fusion) | data formatting | bytes 25165824 | tf_op jit(solution)/shard_map/convert_element_type | solution.py:37
  142.5 0.0 copy-start.1
  142.5 0.0 reduce-scatter.2.cloned.1.call-update
  142.5 75.2 %reduce-scatter.2.cloned.1.call-done = bf16[24,4,32,256]{3,0,1,2:T(8,128)(2,1)} async-done(((bf16[24,4,256,256]{3,0,1,2:T(8,128)(2,1)}), bf16[24,4,32,256]{3,0,1,2:T(8,128)(2,1)}) %reduce-scatter.2.cloned.1.call-update) | async-done | bytes 1572880 | tf_op jit(solution)/shard_map/reduce_scatter | solution.py:36
  217.7 3.4 %copy.20 = bf16[24,4,32,256]{3,2,1,0:T(8,128)(2,1)} copy(bf16[24,4,32,256]{3,0,1,2:T(8,128)(2,1)} %reduce-scatter.2.cloned.1.call-done) | data formatting | bytes 3145728 | tf_op jit(solution)/shard_map/reduce_scatter | solution.py:36
  221.1 0.0 copy-done.1
  (3 shorter events, 0.1 us)
Async XLA Ops:
  6.5 40.2 %copy-start = (f32[1,4,4]{2,1,0:T(4,128)S(1)}, f32[1,4,4]{2,1,0:T(4,128)}, u32[]{:S(2)}) copy-start(f32[1,4,4]{2,1,0:T(4,128)} %param.9) | copy-start | bytes 196
  10.3 14.7 %all-to-all-start = ((s32[16,1,2]{2,1,0:T(1,128)}), s32[16,1,2]{2,1,0:T(1,128)S(1)}, u32[]{:S(2)}, u32[]{:S(2)}) async-start(s32[16,1,2]{2,1,0:T(1,128)} %bitcast.12), calls=%async_computation | async-start | bytes 16384 | tf_op jit(solution)/shard_map/all_to_all | solution.py:21
  28.9 4.9 %copy-start.2 = (bf16[1,24,256,256]{3,2,1,0:T(8,128)(2,1)S(1)}, bf16[1,24,256,256]{3,2,1,0:T(8,128)(2,1)}, u32[]{:S(2)}) copy-start(bf16[1,24,256,256]{3,2,1,0:T(8,128)(2,1)} %param.11) | copy-start | bytes 9437188
  28.9 83.2 %all-to-all-start.1 = ((bf16[16,2,256,256]{3,2,1,0:T(8,128)(2,1)}), bf16[16,2,256,256]{3,2,1,0:T(8,128)(2,1)}, u32[]{:S(2)}, u32[]{:S(2)}) async-start(bf16[16,2,256,256]{3,2,1,0:T(8,128)(2,1)} %bitcast.41), calls=%async_computation.1 | async-start | bytes 8388608 | tf_op jit(solution)/shard_map/all_to_all | solution.py:26
  33.8 183.9 %reduce-scatter.2.cloned.1.call-start = ((), (), s32[]{:S(2)}) async-start(), calls=%async_computation.3 | async-start | bytes 14155776 | tf_op jit(solution)/shard_map/reduce_scatter | solution.py:36
  142.5 78.7 %copy-start.1 = (f32[1,4,4]{2,1,0:T(4,128)S(1)}, f32[1,4,4]{2,1,0:T(4,128)}, u32[]{:S(2)}) copy-start(f32[1,4,4]{2,1,0:T(4,128)} %param.9) | copy-start | bytes 196
Sparse Core Ops, SparseCore 0:
  142.6 75.0 reduce-scatter.1

commit v2 on v1

v2 whole, which is shorter than its diff:
```python
import functools

import jax
import jax.numpy as jnp
from jax import lax
from jax.experimental import pallas as pl
from jax.experimental.pallas import tpu as pltpu
from jax.sharding import PartitionSpec as P

MESH = pl.DeviceIdType.MESH
F32 = jnp.float32
BF16 = jnp.bfloat16

Z = 4
SIDE = 4
OWNERS = SIDE * SIDE
CAP = 2
PHASES = Z
GROUPS = 4
EARLY = 6
OFFSETS = [(dx, dy) for dx in range(SIDE) for dy in range(SIDE) if dx or dy]


def kernel(
    mpo, left_dims, right_dims, dest, slot, left_ref, psi_hbm, right_hbm, out_ref,
    left_kept, table, tables, table_smem, slot_smem, stage, arr0, arr1, arr2, arr3,
    mixed, psi_buf, right_buf, mine, give0, give1, give2, give3, got0, got1, got2, got3,
    ring_out0, ring_out1, ring_out2, ring_in0, ring_in1, ring_in2,
    tab_send, tab_recv, tab_local, a_send, a_recv, p_sem, r_sem, g_send, g_recv, n_send, n_recv,
):
    blocks, states, width = psi_hbm.shape[0], psi_hbm.shape[1], psi_hbm.shape[2]
    sectors = left_ref.shape[1]
    rows = width // (2 * Z)
    per = blocks // GROUPS
    arrived = (arr0, arr1, arr2, arr3)
    give = (give0, give1, give2, give3)
    got = (got0, got1, got2, got3)
    ring_out = (ring_out0, ring_out1, ring_out2)
    ring_in = (ring_in0, ring_in1, ring_in2)

    chan = lax.axis_index("chan")
    me = lax.axis_index("sec")
    z, core = chan // 2, lax.rem(chan, 2)
    y, x = me // SIDE, lax.rem(me, SIDE)
    up = lax.rem(z + 1 + 2 * core, Z) * 2 + core
    down = lax.rem(z + 3 + 2 * core, Z) * 2 + core
    partner = z * 2 + 1 - core

    def away(dx, dy):
        return lax.rem(y + dy, SIDE) * SIDE + lax.rem(x + dx, SIDE)

    barrier = pltpu.get_barrier_semaphore()
    for dx, dy in OFFSETS:
        pl.semaphore_signal(barrier, inc=1, device_id=(chan, away(dx, dy)), device_id_type=MESH)
    for other in (down, partner):
        pl.semaphore_signal(barrier, inc=1, device_id=(other, me), device_id_type=MESH)

    def fetch(k, b):
        pltpu.make_async_copy(psi_hbm.at[k], psi_buf.at[b], p_sem.at[b]).start()
        pltpu.make_async_copy(right_hbm.at[0, k], right_buf.at[b], r_sem.at[b]).start()

    fetch(0, 0)

    lane = lax.broadcasted_iota(jnp.int32, (1, 128), 1)
    lane_owner, lane_place = lane // CAP, lax.rem(lane, CAP)
    wanted = jnp.zeros((1, 128), jnp.int32)
    count = jnp.zeros((1, 128), jnp.int32)
    for k in range(blocks):
        own = lane_owner == dest[k, 0]
        wanted = jnp.where(own & (count == lane_place), slot[k], wanted)
        count = count + jnp.where(own, 1, 0)
    table[...] = wanted

    for k in range(blocks):
        place = dest[k, 0] * CAP
        for before in range(k):
            place = place + jnp.where(dest[before, 0] == dest[k, 0], 1, 0)
        slot_smem[k] = place

    row_at = lax.broadcasted_iota(jnp.int32, (width, width), 0)
    col_at = lax.broadcasted_iota(jnp.int32, (width, width), 1)

    def kept(values, dim):
        mask = jnp.where((row_at < dim) & (col_at < dim), 1.0, 0.0).astype(BF16)
        return values * mask

    def keep_left(s, _):
        left_kept[s] = kept(left_ref[0, s], left_dims[s])
        return 0

    lax.fori_loop(0, sectors, keep_left, 0)

    pl.semaphore_wait(barrier, len(OFFSETS) + 2)

    asks = []
    for o, (dx, dy) in enumerate(OFFSETS):
        asks.append(
            pltpu.make_async_remote_copy(
                src_ref=table, dst_ref=tables.at[o], send_sem=tab_send.at[o],
                recv_sem=tab_recv.at[o], device_id=(chan, away(dx, dy)), device_id_type=MESH,
            )
        )
        asks[-1].start()
    tables[OWNERS - 1] = wanted

    def mix(k, _):
        b = lax.rem(k, 2)

        @pl.when(k + 1 < blocks)
        def _():
            fetch(k + 1, 1 - b)

        pltpu.make_async_copy(psi_hbm.at[k], psi_buf.at[b], p_sem.at[b]).wait()
        pltpu.make_async_copy(right_hbm.at[0, k], right_buf.at[b], r_sem.at[b]).wait()
        right = kept(right_buf[b], right_dims[k])
        inner = lax.dot_general(
            psi_buf[b].reshape(states * width, width), right, (((1,), (1,)), ((), ())),
            preferred_element_type=F32,
        )
        for s in range(states):
            total = mpo[0, s, 0] * inner[:width]
            for p in range(1, states):
                total = total + mpo[0, s, p] * inner[p * width : (p + 1) * width]
            mixed[k, :, s * width : (s + 1) * width] = total.astype(BF16)
        return 0

    lax.fori_loop(0, EARLY, mix, 0)

    for ask in asks:
        ask.wait_recv()
    local = pltpu.make_async_copy(tables, table_smem, tab_local)
    local.start()
    local.wait()

    def first_row(p, c):
        chip = jnp.where(c == 0, lax.rem(z + 3 - p + Z, Z), lax.rem(z + 1 + p, Z))
        return pl.multiple_of((chip * 2 + c) * rows, rows)

    sends = []
    for p in range(PHASES):
        own_row, other_row = first_row(p, core), first_row(p, 1 - core)

        def put(o, _, own_row=own_row, other_row=other_row, p=p):
            for q in range(CAP):
                s = table_smem[o, 0, CAP * me + q]
                stage[p, o, q, :rows] = left_kept[s, pl.ds(own_row, rows), :]
                stage[p, o, q, rows:] = left_kept[s, pl.ds(other_row, rows), :]
            return 0

        lax.fori_loop(0, OWNERS - 1, put, 0)
        for o, (dx, dy) in enumerate(OFFSETS):
            sends.append(
                pltpu.make_async_remote_copy(
                    src_ref=stage.at[p, o], dst_ref=arrived[p].at[pl.ds(CAP * me, CAP)],
                    send_sem=a_send.at[p, o], recv_sem=a_recv.at[p, o],
                    device_id=(chan, away(SIDE - dx, SIDE - dy)), device_id_type=MESH,
                )
            )
            sends[-1].start()
        for q in range(CAP):
            s = table_smem[OWNERS - 1, 0, CAP * me + q]
            arrived[p][CAP * me + q, :rows] = left_kept[s, pl.ds(own_row, rows), :]
            arrived[p][CAP * me + q, rows:] = left_kept[s, pl.ds(other_row, rows), :]

    lax.fori_loop(EARLY, blocks, mix, 0)

    others = []

    def apply_left(p, g):
        def one(k, _):
            term = jnp.dot(arrived[p][slot_smem[k]], mixed[k], preferred_element_type=F32)
            mine[k] = term[:rows]
            give[p][k] = term[rows:].astype(BF16)
            return 0

        lax.fori_loop(g * per, (g + 1) * per, one, 0)
        part = pl.ds(g * per, per)
        copy = pltpu.make_async_remote_copy(
            src_ref=give[p].at[part], dst_ref=got[p].at[part], send_sem=g_send.at[p, g],
            recv_sem=g_recv.at[p, g], device_id=(partner, me), device_id_type=MESH,
        )
        copy.start()
        others.append(copy)
        return copy

    hops = {}

    def combine(p, g, copy):
        copy.wait_recv()
        if p:
            hops[p - 1, g].wait_recv()

        def one(k, _):
            total = mine[k] + got[p][k].astype(F32)
            if p:
                total = total + ring_in[p - 1][k].astype(F32)
            total = total.astype(BF16)
            if p < PHASES - 1:
                ring_out[p][k] = total
            else:
                for s in range(states):
                    out_ref[k, s] = total[:, s * width : (s + 1) * width]
            return 0

        lax.fori_loop(g * per, (g + 1) * per, one, 0)
        if p < PHASES - 1:
            part = pl.ds(g * per, per)
            hops[p, g] = pltpu.make_async_remote_copy(
                src_ref=ring_out[p].at[part], dst_ref=ring_in[p].at[part],
                send_sem=n_send.at[p, g], recv_sem=n_recv.at[p, g],
                device_id=(up, me), device_id_type=MESH,
            )
            hops[p, g].start()

    for p in range(PHASES):
        for o in range(OWNERS - 1):
            sends[p * (OWNERS - 1) + o].wait_recv()
        copies = []
        for g in range(GROUPS):
            copies.append(apply_left(p, g))
            if g:
                combine(p, g - 1, copies[g - 1])
        combine(p, GROUPS - 1, copies[GROUPS - 1])

    for copy in asks + sends + others + list(hops.values()):
        copy.wait_send()


def on_device(psi, mpo, left_env, right_env, left_dims, right_dims, dest_owner, left_slot):
    blocks, states, width = psi.shape[0], psi.shape[1], psi.shape[2]
    sectors = left_env.shape[1]
    rows = width // (2 * Z)
    wide = states * width
    smem = pl.BlockSpec(memory_space=pltpu.SMEM)
    vmem = pl.BlockSpec(memory_space=pltpu.VMEM)
    hbm = pl.BlockSpec(memory_space=pl.ANY)
    dma = pltpu.SemaphoreType.DMA
    piece = pltpu.VMEM((blocks, rows, wide), BF16)
    return pl.pallas_call(
        kernel,
        out_shape=jax.ShapeDtypeStruct((blocks, states, rows, width), BF16),
        in_specs=[smem] * 5 + [vmem, hbm, hbm],
        out_specs=vmem,
        scratch_shapes=[
            pltpu.VMEM((sectors, width, width), BF16),
            pltpu.VMEM((1, 128), jnp.int32),
            pltpu.VMEM((OWNERS, 1, 128), jnp.int32),
            pltpu.SMEM((OWNERS, 1, 128), jnp.int32),
            pltpu.SMEM((blocks,), jnp.int32),
            pltpu.VMEM((PHASES, OWNERS - 1, CAP, 2 * rows, width), BF16),
            *[pltpu.VMEM((OWNERS * CAP, 2 * rows, width), BF16)] * PHASES,
            pltpu.VMEM((blocks, width, wide), BF16),
            pltpu.VMEM((2, states, width, width), BF16),
            pltpu.VMEM((2, width, width), BF16),
            pltpu.VMEM((blocks, rows, wide), F32),
            *[piece] * (2 * PHASES + 2 * (PHASES - 1)),
            dma((OWNERS - 1,)),
            dma((OWNERS - 1,)),
            dma,
            dma((PHASES, OWNERS - 1)),
            dma((PHASES, OWNERS - 1)),
            dma((2,)),
            dma((2,)),
            dma((PHASES, GROUPS)),
            dma((PHASES, GROUPS)),
            dma((PHASES - 1, GROUPS)),
            dma((PHASES - 1, GROUPS)),
        ],
        compiler_params=pltpu.CompilerParams(
            collective_id=0, has_side_effects=True, vmem_limit_bytes=67043328
        ),
    )(mpo, left_dims, right_dims, dest_owner, left_slot, left_env, psi, right_env)


def solution(mesh):
    in_specs = (
        P("sec", None, None, None),
        P("chan", None, None),
        P("chan", "sec", None, None),
        P("chan", "sec", None, None),
        P("sec"),
        P("sec"),
        P("sec", None),
        P("sec"),
    )
    out_specs = P("sec", None, "chan", None)
    return jax.shard_map(
        on_device, mesh=mesh, in_specs=in_specs, out_specs=out_specs, check_vma=False
    )
```

time: 229 us -> 98 us (0.43)
  the two profiles are of different devices: /device:TPU:0 before, /device:TPU:24 now
where the time goes in v2:
time: 98 us; the launch traced here: 97.5 us
  Pallas kernels  93.4 us (95%)
  local copies, waits for them, and re-layouts  4.08 us (4%)
    pallas_call x1, Pallas kernels, on_device(): pl.pallas_call(kernel, out_shape=jax.ShapeDtypeStruct((blocks, states, ro...  93.4 us
    unnamed x2, local copies, waits for them, and re-layouts  4.08 us

profile of v2, /device:TPU:24, one launch (start us, length us, event | category | flops | bytes accessed | tf_op | source)
XLA Modules:
  0.0 97.5 jit_solution(4423703657878052962)
XLA Ops:
  0.0 1.3 %copy.9.dest = s32[24,1]{1,0:T(8,128)} copy(s32[24,1]{0,1:T(1,128)} %param.14) | data formatting | bytes 192 | tf_op args[6]
  1.3 93.4 %shard_map.82 = bf16[24,4,32,256]{3,2,1,0:T(8,128)(2,1)} custom-call(f32[1,4,4]{2,1,0:T(4,128)} %mpo.1, s32[8]{0:T(128)} %left_dims.1, s32[24]{0:T(128)} %right_dims.1, s32[24,1]{1,0:T(8,128)} %copy.9.dest, s32[24]{0:T(128)} %slot.1, bf16[1,8,256,256]{3,2,1,0:T(8,128)(2,1)} %left_ref.1, bf16[24,4,256,256]{3,2,1,0:T(8,128)(2,1)} %psi_hbm.1, ...), custom_call_target="tpu_custom_call" | custom-call | tf_op jit(solution)/shard_map/pallas_call | solution.py:239
  94.8 2.7 %copy.11 = bf16[24,4,32,256]{3,2,1,0:T(8,128)(2,1)} copy(bf16[24,4,32,256]{3,2,1,0:T(8,128)(2,1)} %shard_map.82) | data formatting | bytes 3145728

commit v3 on v2

v3 whole, which is shorter than its diff:
```python
import functools

import jax
import jax.numpy as jnp
from jax import lax
from jax.experimental import pallas as pl
from jax.experimental.pallas import tpu as pltpu
from jax.sharding import PartitionSpec as P

MESH = pl.DeviceIdType.MESH
F32 = jnp.float32
BF16 = jnp.bfloat16

Z = 4
SIDE = 4
OWNERS = SIDE * SIDE
CAP = 2
PHASES = Z
GROUPS = 4
PSI_READ = 2
RIGHT_READ = 4
ASKING = 5
ALONE = 7
BEFORE = 14
CHUNKS = ((0, 0, 16), (0, 16, 16), (1, 0, 32), (2, 0, 32), (3, 0, 32))
OFFSETS = (
    (1, 0), (0, 1), (3, 0), (0, 3), (1, 1), (3, 3), (1, 3), (3, 1),
    (2, 0), (0, 2), (2, 1), (1, 2), (2, 3), (3, 2), (2, 2),
)


def kernel(
    mpo, left_dims, right_dims, dest, slot, left_hbm, psi_hbm, right_hbm, out_hbm,
    left_kept, table, tables, table_smem, slot_smem,
    stage0, stage1, stage2, stage3, stage4, arr0, arr1, arr2, arr3, arr4,
    work, right_all, mine, give0, give1, give2, give3, got0, got1, got2, got3,
    ring_out0, ring_out1, ring_out2, ring_in0, ring_in1, ring_in2, out_buf,
    tab_send, tab_recv, tab_local, a_send, a_recv, p_sem, r_sem, l_sem, o_sem,
    g_send, g_recv, n_send, n_recv,
):
    blocks, states, width = psi_hbm.shape[0], psi_hbm.shape[1], psi_hbm.shape[2]
    sectors = left_kept.shape[0]
    rows = width // (2 * Z)
    per = blocks // GROUPS
    stage = (stage0, stage1, stage2, stage3, stage4)
    arrived = (arr0, arr1, arr2, arr3, arr4)
    give = (give0, give1, give2, give3)
    got = (got0, got1, got2, got3)
    ring_out = (ring_out0, ring_out1, ring_out2)
    ring_in = (ring_in0, ring_in1, ring_in2)

    chan = lax.axis_index("chan")
    me = lax.axis_index("sec")
    z, core = chan // 2, lax.rem(chan, 2)
    y, x = me // SIDE, lax.rem(me, SIDE)
    up = lax.rem(z + 1 + 2 * core, Z) * 2 + core
    down = lax.rem(z + 3 + 2 * core, Z) * 2 + core
    partner = z * 2 + 1 - core

    def away(dx, dy):
        return lax.rem(y + dy, SIDE) * SIDE + lax.rem(x + dx, SIDE)

    barrier = pltpu.get_barrier_semaphore()
    for dx, dy in OFFSETS:
        pl.semaphore_signal(barrier, inc=1, device_id=(chan, away(dx, dy)), device_id_type=MESH)
    for other in (down, partner):
        pl.semaphore_signal(barrier, inc=1, device_id=(other, me), device_id_type=MESH)

    def psi_copy(i):
        part = pl.ds(i * PSI_READ, PSI_READ)
        return pltpu.make_async_copy(psi_hbm.at[part], work.at[part], p_sem.at[i])

    def right_copy(i):
        part = pl.ds(i * RIGHT_READ, RIGHT_READ)
        return pltpu.make_async_copy(right_hbm.at[0, part], right_all.at[part], r_sem.at[i])

    def all_of(ref, sem):
        return pltpu.make_async_copy(ref, ref, sem)

    left_copy = pltpu.make_async_copy(left_hbm.at[0], left_kept, l_sem)

    def read(first, last):
        for k in range(first, last):
            if k % RIGHT_READ == 0:
                right_copy(k // RIGHT_READ).start()
            if k % PSI_READ == 0:
                psi_copy(k // PSI_READ).start()

    read(0, ASKING)
    left_copy.start()

    lane = lax.broadcasted_iota(jnp.int32, (1, 128), 1)
    lane_owner, lane_place = lane // CAP, lax.rem(lane, CAP)
    wanted = jnp.zeros((1, 128), jnp.int32)
    count = jnp.zeros((1, 128), jnp.int32)
    for k in range(blocks):
        own = lane_owner == dest[k]
        wanted = jnp.where(own & (count == lane_place), slot[k], wanted)
        count = count + jnp.where(own, 1, 0)
    table[...] = wanted

    pl.semaphore_wait(barrier, len(OFFSETS) + 2)

    for o, (dx, dy) in enumerate(OFFSETS):
        pltpu.make_async_remote_copy(
            src_ref=table, dst_ref=tables.at[o], send_sem=tab_send, recv_sem=tab_recv,
            device_id=(chan, away(dx, dy)), device_id_type=MESH,
        ).start()
    tables[OWNERS - 1] = wanted
    read(ASKING, blocks)

    row_at = lax.broadcasted_iota(jnp.int32, (width, width), 0)
    col_at = lax.broadcasted_iota(jnp.int32, (width, width), 1)

    def kept(values, dim):
        mask = jnp.where((row_at < dim) & (col_at < dim), 1.0, 0.0).astype(BF16)
        return values * mask

    def mix(k, _):
        @pl.when(lax.rem(k, RIGHT_READ) == 0)
        def _():
            right_copy(k // RIGHT_READ).wait()

        @pl.when(lax.rem(k, PSI_READ) == 0)
        def _():
            psi_copy(k // PSI_READ).wait()

        right = kept(right_all[k], right_dims[k])
        inner = lax.dot_general(
            work[k].reshape(states * width, width), right, (((1,), (1,)), ((), ())),
            preferred_element_type=F32,
        )
        for s in range(states):
            total = mpo[0, s, 0] * inner[:width]
            for p in range(1, states):
                total = total + mpo[0, s, p] * inner[p * width : (p + 1) * width]
            work[k, s] = total.astype(BF16)
        return 0

    def keep_left(s, _):
        left_kept[s] = kept(left_kept[s], left_dims[s])
        return 0

    lax.fori_loop(0, ASKING, mix, 0)
    left_copy.wait()
    lax.fori_loop(0, sectors, keep_left, 0)

    all_of(tables.at[pl.ds(0, OWNERS - 1)], tab_recv).wait()
    local = pltpu.make_async_copy(tables, table_smem, tab_local)
    local.start()

    for k in range(blocks):
        place = dest[k] * CAP
        for before in range(k):
            place = place + jnp.where(dest[before] == dest[k], 1, 0)
        slot_smem[k] = place

    local.wait()

    def first_row(p, c):
        chip = jnp.where(c == 0, lax.rem(z + 3 - p + Z, Z), lax.rem(z + 1 + p, Z))
        return (chip * 2 + c) * rows

    def issue(c):
        p, first, num = CHUNKS[c]
        own_row = pl.multiple_of(first_row(p, core) + first, 16)
        other_row = pl.multiple_of(first_row(p, 1 - core) + first, 16)

        def put(o, _):
            for q in range(CAP):
                s = table_smem[o, 0, CAP * me + q]
                stage[c][o, q, :num] = left_kept[s, pl.ds(own_row, num), :]
                stage[c][o, q, num:] = left_kept[s, pl.ds(other_row, num), :]
            return 0

        lax.fori_loop(0, OWNERS - 1, put, 0)
        for o, (dx, dy) in enumerate(OFFSETS):
            pltpu.make_async_remote_copy(
                src_ref=stage[c].at[o], dst_ref=arrived[c].at[pl.ds(CAP * me, CAP)],
                send_sem=a_send.at[c], recv_sem=a_recv.at[c],
                device_id=(chan, away(SIDE - dx, SIDE - dy)), device_id_type=MESH,
            ).start()
        for q in range(CAP):
            s = table_smem[OWNERS - 1, 0, CAP * me + q]
            arrived[c][CAP * me + q, :num] = left_kept[s, pl.ds(own_row, num), :]
            arrived[c][CAP * me + q, num:] = left_kept[s, pl.ds(other_row, num), :]

    issue(0)
    lax.fori_loop(ASKING, ASKING + ALONE, mix, 0)
    issue(1)
    lax.fori_loop(ASKING + ALONE, ASKING + BEFORE, mix, 0)
    issue(2)

    hops, outs = {}, []

    def apply_left(c, g):
        p, first, num = CHUNKS[c]

        def one(k, _):
            lhs = arrived[c][slot_smem[k]]
            for s in range(states):
                term = jnp.dot(lhs, work[k, s], preferred_element_type=F32)
                cols = slice(s * width, (s + 1) * width)
                mine[k, first : first + num, cols] = term[:num]
                give[p][k, first : first + num, cols] = term[num:].astype(BF16)
            return 0

        lax.fori_loop(g * per, (g + 1) * per, one, 0)
        part = (pl.ds(g * per, per), pl.ds(first, num))
        copy = pltpu.make_async_remote_copy(
            src_ref=give[p].at[part], dst_ref=got[p].at[part], send_sem=g_send.at[p],
            recv_sem=g_recv.at[c, g], device_id=(partner, me), device_id_type=MESH,
        )
        copy.start()
        return copy

    def combine(c, g, copy):
        p, first, num = CHUNKS[c]
        copy.wait_recv()
        for before, (q, _, _) in enumerate(CHUNKS):
            if q == p - 1:
                hops[before, g].wait_recv()
        at = slice(first, first + num)

        def one(k, _):
            total = mine[k, at] + got[p][k, at].astype(F32)
            if p:
                total = total + ring_in[p - 1][k, at].astype(F32)
            total = total.astype(BF16)
            if p < PHASES - 1:
                ring_out[p][k, at] = total
            else:
                for s in range(states):
                    out_buf[k, s, at] = total[:, s * width : (s + 1) * width]
            return 0

        lax.fori_loop(g * per, (g + 1) * per, one, 0)
        blocks_of = pl.ds(g * per, per)
        if p < PHASES - 1:
            part = (blocks_of, pl.ds(first, num))
            hops[c, g] = pltpu.make_async_remote_copy(
                src_ref=ring_out[p].at[part], dst_ref=ring_in[p].at[part],
                send_sem=n_send.at[p], recv_sem=n_recv.at[c, g],
                device_id=(up, me), device_id_type=MESH,
            )
            hops[c, g].start()
        else:
            outs.append(
                pltpu.make_async_copy(out_buf.at[blocks_of], out_hbm.at[blocks_of], o_sem.at[g])
            )
            outs[-1].start()

    for c in range(len(CHUNKS)):
        all_of(stage[c], a_recv.at[c]).wait()
        if c == 2:
            issue(4)
        copies = []
        for g in range(GROUPS):
            if c == 0 and g == 2:
                lax.fori_loop(ASKING + BEFORE, blocks, mix, 0)
                issue(3)
            copies.append(apply_left(c, g))
            if g:
                combine(c, g - 1, copies[g - 1])
        combine(c, GROUPS - 1, copies[GROUPS - 1])

    all_of(tables.at[pl.ds(0, OWNERS - 1)], tab_send).wait()
    for c in range(len(CHUNKS)):
        all_of(stage[c], a_send.at[c]).wait()
    for p in range(PHASES):
        all_of(give[p], g_send.at[p]).wait()
    for p in range(PHASES - 1):
        all_of(ring_out[p], n_send.at[p]).wait()
    for copy in outs:
        copy.wait()


def on_device(psi, mpo, left_env, right_env, left_dims, right_dims, dest_owner, left_slot):
    blocks, states, width = psi.shape[0], psi.shape[1], psi.shape[2]
    sectors = left_env.shape[1]
    rows = width // (2 * Z)
    wide = states * width
    chunks = len(CHUNKS)
    smem = pl.BlockSpec(memory_space=pltpu.SMEM)
    hbm = pl.BlockSpec(memory_space=pl.ANY)
    dma = pltpu.SemaphoreType.DMA
    piece = pltpu.VMEM((blocks, rows, wide), BF16)
    return pl.pallas_call(
        kernel,
        out_shape=jax.ShapeDtypeStruct((blocks, states, rows, width), BF16),
        in_specs=[smem] * 5 + [hbm] * 3,
        out_specs=hbm,
        scratch_shapes=[
            pltpu.VMEM((sectors, width, width), BF16),
            pltpu.VMEM((1, 128), jnp.int32),
            pltpu.VMEM((OWNERS, 1, 128), jnp.int32),
            pltpu.SMEM((OWNERS, 1, 128), jnp.int32),
            pltpu.SMEM((blocks,), jnp.int32),
            *[pltpu.VMEM((OWNERS - 1, CAP, 2 * num, width), BF16) for _, _, num in CHUNKS],
            *[pltpu.VMEM((OWNERS * CAP, 2 * num, width), BF16) for _, _, num in CHUNKS],
            pltpu.VMEM((blocks, states, width, width), BF16),
            pltpu.VMEM((blocks, width, width), BF16),
            pltpu.VMEM((blocks, rows, wide), F32),
            *[piece] * (2 * PHASES + 2 * (PHASES - 1)),
            pltpu.VMEM((blocks, states, rows, width), BF16),
            dma,
            dma,
            dma,
            dma((chunks,)),
            dma((chunks,)),
            dma((blocks // PSI_READ,)),
            dma((blocks // RIGHT_READ,)),
            dma,
            dma((GROUPS,)),
            dma((PHASES,)),
            dma((chunks, GROUPS)),
            dma((PHASES - 1,)),
            dma((chunks - 1, GROUPS)),
        ],
        compiler_params=pltpu.CompilerParams(
            collective_id=0, has_side_effects=True, vmem_limit_bytes=67043328
        ),
    )(mpo, left_dims, right_dims, dest_owner.reshape(blocks), left_slot, left_env, psi, right_env)


def solution(mesh):
    in_specs = (
        P("sec", None, None, None),
        P("chan", None, None),
        P("chan", "sec", None, None),
        P("chan", "sec", None, None),
        P("sec"),
        P("sec"),
        P("sec", None),
        P("sec"),
    )
    out_specs = P("sec", None, "chan", None)
    return jax.shard_map(
        on_device, mesh=mesh, in_specs=in_specs, out_specs=out_specs, check_vma=False
    )
```

time: 98 us -> 87.2 us (0.89)
  the two profiles are of different devices: /device:TPU:24 before, /device:TPU:0 now
where the time goes in v3:
time: 87.2 us; the launch traced here: 87.1 us
  Pallas kernels  84.3 us (97%)
  local copies, waits for them, and re-layouts  2.74 us (3%)
    pallas_call x1, Pallas kernels, on_device(): pl.pallas_call(kernel, out_shape=jax.ShapeDtypeStruct((blocks, states, ro...  84.3 us
    unnamed x1, local copies, waits for them, and re-layouts  2.74 us

profile of v3, /device:TPU:0, one launch (start us, length us, event | category | flops | bytes accessed | tf_op | source)
XLA Modules:
  0.0 87.1 jit_solution(10433193758991005813)
XLA Ops:
  0.0 84.3 %shard_map.82 = bf16[24,4,32,256]{3,2,1,0:T(8,128)(2,1)} custom-call(f32[1,4,4]{2,1,0:T(4,128)} %mpo.1, s32[8]{0:T(128)} %left_dims.1, s32[24]{0:T(128)} %right_dims.1, s32[24]{0:T(128)} %bitcast.1, s32[24]{0:T(128)} %slot.1, bf16[1,8,256,256]{3,2,1,0:T(8,128)(2,1)} %left_hbm.1, bf16[24,4,256,256]{3,2,1,0:T(8,128)(2,1)} %psi_hbm.1, ...), custom_call_target="tpu_custom_call" | custom-call | tf_op jit(solution)/shard_map/pallas_call | solution.py:288
  84.3 2.7 %copy.10 = bf16[24,4,32,256]{3,2,1,0:T(8,128)(2,1)} copy(bf16[24,4,32,256]{3,2,1,0:T(8,128)(2,1)} %shard_map.82) | data formatting | bytes 3145728

commit v4 on v3

--- a/solution.py
+++ b/solution.py
@@ -21,7 +21,7 @@
 RIGHT_READ = 4
 ASKING = 5
 ALONE = 7
-BEFORE = 14
+BEFORE = 16
 CHUNKS = ((0, 0, 16), (0, 16, 16), (1, 0, 32), (2, 0, 32), (3, 0, 32))
 OFFSETS = (
     (1, 0), (0, 1), (3, 0), (0, 3), (1, 1), (3, 3), (1, 3), (3, 1),
@@ -30,12 +30,12 @@
 
 
 def kernel(
-    mpo, left_dims, right_dims, dest, slot, left_hbm, psi_hbm, right_hbm, out_hbm,
-    left_kept, table, tables, table_smem, slot_smem,
+    mpo, left_dims, right_dims, dest, slot, left_hbm, psi_hbm, right_hbm, out_ref,
+    left_kept, table, asked, slot_smem,
     stage0, stage1, stage2, stage3, stage4, arr0, arr1, arr2, arr3, arr4,
     work, right_all, mine, give0, give1, give2, give3, got0, got1, got2, got3,
-    ring_out0, ring_out1, ring_out2, ring_in0, ring_in1, ring_in2, out_buf,
-    tab_send, tab_recv, tab_local, a_send, a_recv, p_sem, r_sem, l_sem, o_sem,
+    ring_out0, ring_out1, ring_out2, ring_in0, ring_in1, ring_in2,
+    tab_send, tab_recv, tab_local, a_send, a_recv, p_sem, r_sem, l_sem,
     g_send, g_recv, n_send, n_recv,
 ):
     blocks, states, width = psi_hbm.shape[0], psi_hbm.shape[1], psi_hbm.shape[2]
@@ -103,10 +103,11 @@
 
     for o, (dx, dy) in enumerate(OFFSETS):
         pltpu.make_async_remote_copy(
-            src_ref=table, dst_ref=tables.at[o], send_sem=tab_send, recv_sem=tab_recv,
+            src_ref=table, dst_ref=asked.at[o], send_sem=tab_send, recv_sem=tab_recv,
             device_id=(chan, away(dx, dy)), device_id_type=MESH,
         ).start()
-    tables[OWNERS - 1] = wanted
+    own_ask = pltpu.make_async_copy(table, asked.at[OWNERS - 1], tab_local)
+    own_ask.start()
     read(ASKING, blocks)
 
     row_at = lax.broadcasted_iota(jnp.int32, (width, width), 0)
@@ -145,9 +146,7 @@
     left_copy.wait()
     lax.fori_loop(0, sectors, keep_left, 0)
 
-    all_of(tables.at[pl.ds(0, OWNERS - 1)], tab_recv).wait()
-    local = pltpu.make_async_copy(tables, table_smem, tab_local)
-    local.start()
+    all_of(asked.at[pl.ds(0, OWNERS - 1)], tab_recv).wait()
 
     for k in range(blocks):
         place = dest[k] * CAP
@@ -155,7 +154,7 @@
             place = place + jnp.where(dest[before] == dest[k], 1, 0)
         slot_smem[k] = place
 
-    local.wait()
+    own_ask.wait()
 
     def first_row(p, c):
         chip = jnp.where(c == 0, lax.rem(z + 3 - p + Z, Z), lax.rem(z + 1 + p, Z))
@@ -168,7 +167,7 @@
 
         def put(o, _):
             for q in range(CAP):
-                s = table_smem[o, 0, CAP * me + q]
+                s = asked[o, 0, CAP * me + q]
                 stage[c][o, q, :num] = left_kept[s, pl.ds(own_row, num), :]
                 stage[c][o, q, num:] = left_kept[s, pl.ds(other_row, num), :]
             return 0
@@ -181,7 +180,7 @@
                 device_id=(chan, away(SIDE - dx, SIDE - dy)), device_id_type=MESH,
             ).start()
         for q in range(CAP):
-            s = table_smem[OWNERS - 1, 0, CAP * me + q]
+            s = asked[OWNERS - 1, 0, CAP * me + q]
             arrived[c][CAP * me + q, :num] = left_kept[s, pl.ds(own_row, num), :]
             arrived[c][CAP * me + q, num:] = left_kept[s, pl.ds(other_row, num), :]
 
@@ -191,7 +190,7 @@
     lax.fori_loop(ASKING + ALONE, ASKING + BEFORE, mix, 0)
     issue(2)
 
-    hops, outs = {}, []
+    hops = {}
 
     def apply_left(c, g):
         p, first, num = CHUNKS[c]
@@ -231,7 +230,7 @@
                 ring_out[p][k, at] = total
             else:
                 for s in range(states):
-                    out_buf[k, s, at] = total[:, s * width : (s + 1) * width]
+                    out_ref[k, s, at] = total[:, s * width : (s + 1) * width]
             return 0
 
         lax.fori_loop(g * per, (g + 1) * per, one, 0)
@@ -244,11 +243,6 @@
                 device_id=(up, me), device_id_type=MESH,
             )
             hops[c, g].start()
-        else:
-            outs.append(
-                pltpu.make_async_copy(out_buf.at[blocks_of], out_hbm.at[blocks_of], o_sem.at[g])
-            )
-            outs[-1].start()
 
     for c in range(len(CHUNKS)):
         all_of(stage[c], a_recv.at[c]).wait()
@@ -256,23 +250,24 @@
             issue(4)
         copies = []
         for g in range(GROUPS):
-            if c == 0 and g == 2:
+            copies.append(apply_left(c, g))
+            if c == 0 and g == 1:
+                combine(c, 0, copies[0])
                 lax.fori_loop(ASKING + BEFORE, blocks, mix, 0)
+                combine(c, 1, copies[1])
+            elif c == 0 and g == 2:
                 issue(3)
-            copies.append(apply_left(c, g))
-            if g:
+            elif g:
                 combine(c, g - 1, copies[g - 1])
         combine(c, GROUPS - 1, copies[GROUPS - 1])
 
-    all_of(tables.at[pl.ds(0, OWNERS - 1)], tab_send).wait()
+    all_of(asked.at[pl.ds(0, OWNERS - 1)], tab_send).wait()
     for c in range(len(CHUNKS)):
         all_of(stage[c], a_send.at[c]).wait()
     for p in range(PHASES):
         all_of(give[p], g_send.at[p]).wait()
     for p in range(PHASES - 1):
         all_of(ring_out[p], n_send.at[p]).wait()
-    for copy in outs:
-        copy.wait()
 
 
 def on_device(psi, mpo, left_env, right_env, left_dims, right_dims, dest_owner, left_slot):
@@ -287,13 +282,12 @@
     piece = pltpu.VMEM((blocks, rows, wide), BF16)
     return pl.pallas_call(
         kernel,
-        out_shape=jax.ShapeDtypeStruct((blocks, states, rows, width), BF16),
+        out_shape=pltpu.VMEM((blocks, states, rows, width), BF16),
         in_specs=[smem] * 5 + [hbm] * 3,
-        out_specs=hbm,
+        out_specs=pl.BlockSpec(memory_space=pltpu.VMEM),
         scratch_shapes=[
             pltpu.VMEM((sectors, width, width), BF16),
             pltpu.VMEM((1, 128), jnp.int32),
-            pltpu.VMEM((OWNERS, 1, 128), jnp.int32),
             pltpu.SMEM((OWNERS, 1, 128), jnp.int32),
             pltpu.SMEM((blocks,), jnp.int32),
             *[pltpu.VMEM((OWNERS - 1, CAP, 2 * num, width), BF16) for _, _, num in CHUNKS],
@@ -302,7 +296,6 @@
             pltpu.VMEM((blocks, width, width), BF16),
             pltpu.VMEM((blocks, rows, wide), F32),
             *[piece] * (2 * PHASES + 2 * (PHASES - 1)),
-            pltpu.VMEM((blocks, states, rows, width), BF16),
             dma,
             dma,
             dma,
@@ -311,14 +304,13 @@
             dma((blocks // PSI_READ,)),
             dma((blocks // RIGHT_READ,)),
             dma,
-            dma((GROUPS,)),
             dma((PHASES,)),
             dma((chunks, GROUPS)),
             dma((PHASES - 1,)),
             dma((chunks - 1, GROUPS)),
         ],
         compiler_params=pltpu.CompilerParams(
-            collective_id=0, has_side_effects=True, vmem_limit_bytes=67043328
+            collective_id=0, has_side_effects=True, vmem_limit_bytes=58 << 20
         ),
     )(mpo, left_dims, right_dims, dest_owner.reshape(blocks), left_slot, left_env, psi, right_env)
 

time: 87.2 us -> 82.7 us (0.948)
  Pallas kernels: 84.3 us -> 81.5 us
  local copies, waits for them, and re-layouts: 2.74 us -> 1.15 us
    pallas_call x1, Pallas kernels: 84.3 us -> 81.5 us  [on_device(): pl.pallas_call(kernel, out_shape=pltpu.VMEM((blocks, states, rows, width)...]
    unnamed x1, local copies, waits for them, and re-layouts: 2.74 us -> 1.15 us
where the time goes in v4:
time: 82.7 us; the launch traced here: 82.6 us
  Pallas kernels  81.5 us (99%)
  local copies, waits for them, and re-layouts  1.15 us (1%)
    pallas_call x1, Pallas kernels, on_device(): pl.pallas_call(kernel, out_shape=pltpu.VMEM((blocks, states, rows, width)...  81.5 us

profile of v4, /device:TPU:0, one launch (start us, length us, event | category | flops | bytes accessed | tf_op | source)
XLA Modules:
  0.0 82.6 jit_solution(10853337677693480694)
XLA Ops:
  0.0 81.5 %shard_map.82 = bf16[24,4,32,256]{3,2,1,0:T(8,128)(2,1)S(1)} custom-call(f32[1,4,4]{2,1,0:T(4,128)} %mpo.1, s32[8]{0:T(128)} %left_dims.1, s32[24]{0:T(128)} %right_dims.1, s32[24]{0:T(128)} %bitcast.1, s32[24]{0:T(128)} %slot.1, bf16[1,8,256,256]{3,2,1,0:T(8,128)(2,1)} %left_hbm.1, bf16[24,4,256,256]{3,2,1,0:T(8,128)(2,1)} %psi_hbm.1, ...), custom_call_target="tpu_custom_call" | custom-call | tf_op jit(solution)/shard_map/pallas_call | solution.py:283
  81.5 1.1 %copy.10 = bf16[24,4,32,256]{3,2,1,0:T(8,128)(2,1)} copy(bf16[24,4,32,256]{3,2,1,0:T(8,128)(2,1)S(1)} %shard_map.82) | data formatting | bytes 3145728

commit v5 on v4

--- a/solution.py
+++ b/solution.py
@@ -16,13 +16,15 @@
 OWNERS = SIDE * SIDE
 CAP = 2
 PHASES = Z
-GROUPS = 4
 PSI_READ = 2
 RIGHT_READ = 4
-ASKING = 5
-ALONE = 7
-BEFORE = 16
-CHUNKS = ((0, 0, 16), (0, 16, 16), (1, 0, 32), (2, 0, 32), (3, 0, 32))
+ASKING = 7
+ALONE = 8
+BEFORE = 14
+CHUNKS = ((0, 0, 16), (0, 16, 16), (1, 0, 16), (1, 16, 16), (2, 0, 32), (3, 0, 32))
+EVEN = ((0, 6), (6, 6), (12, 6), (18, 6))
+PIECES = (((0, 3), (3, 3), (6, 6), (12, 6), (18, 6)),) + (EVEN,) * (len(CHUNKS) - 1)
+MOST = max(len(pieces) for pieces in PIECES)
 OFFSETS = (
     (1, 0), (0, 1), (3, 0), (0, 3), (1, 1), (3, 3), (1, 3), (3, 1),
     (2, 0), (0, 2), (2, 1), (1, 2), (2, 3), (3, 2), (2, 2),
@@ -30,20 +32,20 @@
 
 
 def kernel(
-    mpo, left_dims, right_dims, dest, slot, left_hbm, psi_hbm, right_hbm, out_ref,
-    left_kept, table, asked, slot_smem,
-    stage0, stage1, stage2, stage3, stage4, arr0, arr1, arr2, arr3, arr4,
+    mpo_hbm, left_dims_hbm, right_dims_hbm, dest_hbm, slot_hbm,
+    left_hbm, psi_hbm, right_hbm, out_ref,
+    mpo, left_dims, right_dims, dest, slot, left_kept, table, asked, slot_smem,
+    stage0, stage1, stage2, stage3, stage4, stage5, arr0, arr1, arr2, arr3, arr4, arr5,
     work, right_all, mine, give0, give1, give2, give3, got0, got1, got2, got3,
     ring_out0, ring_out1, ring_out2, ring_in0, ring_in1, ring_in2,
-    tab_send, tab_recv, tab_local, a_send, a_recv, p_sem, r_sem, l_sem,
+    s_sem, tab_send, tab_recv, tab_local, a_send, a_recv, p_sem, r_sem, l_sem,
     g_send, g_recv, n_send, n_recv,
 ):
     blocks, states, width = psi_hbm.shape[0], psi_hbm.shape[1], psi_hbm.shape[2]
     sectors = left_kept.shape[0]
     rows = width // (2 * Z)
-    per = blocks // GROUPS
-    stage = (stage0, stage1, stage2, stage3, stage4)
-    arrived = (arr0, arr1, arr2, arr3, arr4)
+    stage = (stage0, stage1, stage2, stage3, stage4, stage5)
+    arrived = (arr0, arr1, arr2, arr3, arr4, arr5)
     give = (give0, give1, give2, give3)
     got = (got0, got1, got2, got3)
     ring_out = (ring_out0, ring_out1, ring_out2)
@@ -61,10 +63,20 @@
         return lax.rem(y + dy, SIDE) * SIDE + lax.rem(x + dx, SIDE)
 
     barrier = pltpu.get_barrier_semaphore()
-    for dx, dy in OFFSETS:
+    for dx, dy in OFFSETS[::-1]:
         pl.semaphore_signal(barrier, inc=1, device_id=(chan, away(dx, dy)), device_id_type=MESH)
     for other in (down, partner):
         pl.semaphore_signal(barrier, inc=1, device_id=(other, me), device_id_type=MESH)
+
+    small = [
+        pltpu.make_async_copy(source, target, s_sem.at[i])
+        for i, (source, target) in enumerate(
+            ((dest_hbm, dest), (slot_hbm, slot), (right_dims_hbm, right_dims),
+             (left_dims_hbm, left_dims), (mpo_hbm, mpo))
+        )
+    ]
+    for copy in small:
+        copy.start()
 
     def psi_copy(i):
         part = pl.ds(i * PSI_READ, PSI_READ)
@@ -91,6 +103,8 @@
 
     lane = lax.broadcasted_iota(jnp.int32, (1, 128), 1)
     lane_owner, lane_place = lane // CAP, lax.rem(lane, CAP)
+    small[0].wait()
+    small[1].wait()
     wanted = jnp.zeros((1, 128), jnp.int32)
     count = jnp.zeros((1, 128), jnp.int32)
     for k in range(blocks):
@@ -101,7 +115,7 @@
 
     pl.semaphore_wait(barrier, len(OFFSETS) + 2)
 
-    for o, (dx, dy) in enumerate(OFFSETS):
+    for o, (dx, dy) in list(enumerate(OFFSETS))[::-1]:
         pltpu.make_async_remote_copy(
             src_ref=table, dst_ref=asked.at[o], send_sem=tab_send, recv_sem=tab_recv,
             device_id=(chan, away(dx, dy)), device_id_type=MESH,
@@ -142,17 +156,13 @@
         left_kept[s] = kept(left_kept[s], left_dims[s])
         return 0
 
+    for copy in small[2:]:
+        copy.wait()
     lax.fori_loop(0, ASKING, mix, 0)
     left_copy.wait()
     lax.fori_loop(0, sectors, keep_left, 0)
 
     all_of(asked.at[pl.ds(0, OWNERS - 1)], tab_recv).wait()
-
-    for k in range(blocks):
-        place = dest[k] * CAP
-        for before in range(k):
-            place = place + jnp.where(dest[before] == dest[k], 1, 0)
-        slot_smem[k] = place
 
     own_ask.wait()
 
@@ -185,6 +195,12 @@
             arrived[c][CAP * me + q, num:] = left_kept[s, pl.ds(other_row, num), :]
 
     issue(0)
+    for k in range(blocks):
+        place = dest[k] * CAP
+        for before in range(k):
+            place = place + jnp.where(dest[before] == dest[k], 1, 0)
+        slot_smem[k] = place
+
     lax.fori_loop(ASKING, ASKING + ALONE, mix, 0)
     issue(1)
     lax.fori_loop(ASKING + ALONE, ASKING + BEFORE, mix, 0)
@@ -194,6 +210,7 @@
 
     def apply_left(c, g):
         p, first, num = CHUNKS[c]
+        start, size = PIECES[c][g]
 
         def one(k, _):
             lhs = arrived[c][slot_smem[k]]
@@ -204,8 +221,8 @@
                 give[p][k, first : first + num, cols] = term[num:].astype(BF16)
             return 0
 
-        lax.fori_loop(g * per, (g + 1) * per, one, 0)
-        part = (pl.ds(g * per, per), pl.ds(first, num))
+        lax.fori_loop(start, start + size, one, 0)
+        part = (pl.ds(start, size), pl.ds(first, num))
         copy = pltpu.make_async_remote_copy(
             src_ref=give[p].at[part], dst_ref=got[p].at[part], send_sem=g_send.at[p],
             recv_sem=g_recv.at[c, g], device_id=(partner, me), device_id_type=MESH,
@@ -215,10 +232,14 @@
 
     def combine(c, g, copy):
         p, first, num = CHUNKS[c]
+        start, size = PIECES[c][g]
         copy.wait_recv()
-        for before, (q, _, _) in enumerate(CHUNKS):
-            if q == p - 1:
-                hops[before, g].wait_recv()
+        for before, (q, row, many) in enumerate(CHUNKS):
+            for i, (block, count) in enumerate(PIECES[before]):
+                here = block < start + size and start < block + count
+                if q == p - 1 and row < first + num and first < row + many and here:
+                    if (before, i) in hops:
+                        hops.pop((before, i)).wait_recv()
         at = slice(first, first + num)
 
         def one(k, _):
@@ -233,10 +254,9 @@
                     out_ref[k, s, at] = total[:, s * width : (s + 1) * width]
             return 0
 
-        lax.fori_loop(g * per, (g + 1) * per, one, 0)
-        blocks_of = pl.ds(g * per, per)
+        lax.fori_loop(start, start + size, one, 0)
         if p < PHASES - 1:
-            part = (blocks_of, pl.ds(first, num))
+            part = (pl.ds(start, size), pl.ds(first, num))
             hops[c, g] = pltpu.make_async_remote_copy(
                 src_ref=ring_out[p].at[part], dst_ref=ring_in[p].at[part],
                 send_sem=n_send.at[p], recv_sem=n_recv.at[c, g],
@@ -246,20 +266,25 @@
 
     for c in range(len(CHUNKS)):
         all_of(stage[c], a_recv.at[c]).wait()
-        if c == 2:
-            issue(4)
+        if c in (2, 3):
+            issue(c + 2)
         copies = []
-        for g in range(GROUPS):
-            copies.append(apply_left(c, g))
-            if c == 0 and g == 1:
-                combine(c, 0, copies[0])
-                lax.fori_loop(ASKING + BEFORE, blocks, mix, 0)
-                combine(c, 1, copies[1])
-            elif c == 0 and g == 2:
-                issue(3)
-            elif g:
-                combine(c, g - 1, copies[g - 1])
-        combine(c, GROUPS - 1, copies[GROUPS - 1])
+        if c == 0:
+            copies = [apply_left(c, g) for g in range(3)]
+            combine(c, 0, copies[0])
+            combine(c, 1, copies[1])
+            lax.fori_loop(ASKING + BEFORE, blocks, mix, 0)
+            combine(c, 2, copies[2])
+            copies += [apply_left(c, g) for g in (3, 4)]
+            combine(c, 3, copies[3])
+            combine(c, 4, copies[4])
+            issue(3)
+        else:
+            for g in range(len(PIECES[c])):
+                copies.append(apply_left(c, g))
+                if g:
+                    combine(c, g - 1, copies[g - 1])
+            combine(c, len(PIECES[c]) - 1, copies[-1])
 
     all_of(asked.at[pl.ds(0, OWNERS - 1)], tab_send).wait()
     for c in range(len(CHUNKS)):
@@ -276,16 +301,20 @@
     rows = width // (2 * Z)
     wide = states * width
     chunks = len(CHUNKS)
-    smem = pl.BlockSpec(memory_space=pltpu.SMEM)
     hbm = pl.BlockSpec(memory_space=pl.ANY)
     dma = pltpu.SemaphoreType.DMA
     piece = pltpu.VMEM((blocks, rows, wide), BF16)
     return pl.pallas_call(
         kernel,
         out_shape=pltpu.VMEM((blocks, states, rows, width), BF16),
-        in_specs=[smem] * 5 + [hbm] * 3,
+        in_specs=[hbm] * 8,
         out_specs=pl.BlockSpec(memory_space=pltpu.VMEM),
         scratch_shapes=[
+            pltpu.SMEM(mpo.shape, F32),
+            pltpu.SMEM((sectors,), jnp.int32),
+            pltpu.SMEM((blocks,), jnp.int32),
+            pltpu.SMEM((blocks,), jnp.int32),
+            pltpu.SMEM((blocks,), jnp.int32),
             pltpu.VMEM((sectors, width, width), BF16),
             pltpu.VMEM((1, 128), jnp.int32),
             pltpu.SMEM((OWNERS, 1, 128), jnp.int32),
@@ -296,6 +325,7 @@
             pltpu.VMEM((blocks, width, width), BF16),
             pltpu.VMEM((blocks, rows, wide), F32),
             *[piece] * (2 * PHASES + 2 * (PHASES - 1)),
+            dma((5,)),
             dma,
             dma,
             dma,
@@ -305,9 +335,9 @@
             dma((blocks // RIGHT_READ,)),
             dma,
             dma((PHASES,)),
-            dma((chunks, GROUPS)),
+            dma((chunks, MOST)),
             dma((PHASES - 1,)),
-            dma((chunks - 1, GROUPS)),
+            dma((chunks - 1, MOST)),
         ],
         compiler_params=pltpu.CompilerParams(
             collective_id=0, has_side_effects=True, vmem_limit_bytes=58 << 20

time: 82.7 us -> 80.1 us (0.969)
  Pallas kernels: 81.5 us -> 78.9 us
    pallas_call x1, Pallas kernels: 81.5 us -> 78.9 us  [on_device(): pl.pallas_call(kernel, out_shape=pltpu.VMEM((blocks, states, rows, width)...]
where the time goes in v5:
time: 80.1 us; the launch traced here: 80 us
  Pallas kernels  78.9 us (99%)
  local copies, waits for them, and re-layouts  1.15 us (1%)
    pallas_call x1, Pallas kernels, on_device(): pl.pallas_call(kernel, out_shape=pltpu.VMEM((blocks, states, rows, width)...  78.9 us

profile of v5, /device:TPU:0, one launch (start us, length us, event | category | flops | bytes accessed | tf_op | source)
XLA Modules:
  0.0 80.0 jit_solution(3085393161492846154)
XLA Ops:
  0.0 78.9 %shard_map.82 = bf16[24,4,32,256]{3,2,1,0:T(8,128)(2,1)S(1)} custom-call(f32[1,4,4]{2,1,0:T(4,128)} %mpo_hbm.1, s32[8]{0:T(128)} %left_dims_hbm.1, s32[24]{0:T(128)} %right_dims_hbm.1, s32[24]{0:T(128)} %bitcast.1, s32[24]{0:T(128)} %slot_hbm.1, bf16[1,8,256,256]{3,2,1,0:T(8,128)(2,1)} %left_hbm.1, bf16[24,4,256,256]{3,2,1,0:T(8,128)(2,1)} %psi_hbm.1, ...), custom_call_target="tpu_custom_call" | custom-call | tf_op jit(solution)/shard_map/pallas_call | solution.py:307
  78.9 1.1 %copy.10 = bf16[24,4,32,256]{3,2,1,0:T(8,128)(2,1)} copy(bf16[24,4,32,256]{3,2,1,0:T(8,128)(2,1)S(1)} %shard_map.82) | data formatting | bytes 3145728

commit v6 on v5

--- a/solution.py
+++ b/solution.py
@@ -19,15 +19,14 @@
 PSI_READ = 2
 RIGHT_READ = 4
 ASKING = 7
-ALONE = 8
+ALONE = 10
 BEFORE = 14
 CHUNKS = ((0, 0, 16), (0, 16, 16), (1, 0, 16), (1, 16, 16), (2, 0, 32), (3, 0, 32))
 EVEN = ((0, 6), (6, 6), (12, 6), (18, 6))
 PIECES = (((0, 3), (3, 3), (6, 6), (12, 6), (18, 6)),) + (EVEN,) * (len(CHUNKS) - 1)
 MOST = max(len(pieces) for pieces in PIECES)
 OFFSETS = (
-    (1, 0), (0, 1), (3, 0), (0, 3), (1, 1), (3, 3), (1, 3), (3, 1),
-    (2, 0), (0, 2), (2, 1), (1, 2), (2, 3), (3, 2), (2, 2),
+    (1, 0), (0, 1), (3, 0), (0, 3), (2, 1), (1, 2), (2, 3), (3, 2), (1, 1), (3, 3), (1, 3), (3, 1), (2, 0), (0, 2), (2, 2),
 )
 
 

time: 80.1 us -> 79.5 us (level)
  no operation moved by 1% of the time
where the time goes in v6:
time: 79.5 us; the launch traced here: 79.4 us
  Pallas kernels  78.2 us (98%)
  local copies, waits for them, and re-layouts  1.15 us (1%)
    pallas_call x1, Pallas kernels, on_device(): pl.pallas_call(kernel, out_shape=pltpu.VMEM((blocks, states, rows, width)...  78.2 us

profile of v6, /device:TPU:0, one launch (start us, length us, event | category | flops | bytes accessed | tf_op | source)
XLA Modules:
  0.0 79.4 jit_solution(17222275707432045614)
XLA Ops:
  0.0 78.2 %shard_map.82 = bf16[24,4,32,256]{3,2,1,0:T(8,128)(2,1)S(1)} custom-call(f32[1,4,4]{2,1,0:T(4,128)} %mpo_hbm.1, s32[8]{0:T(128)} %left_dims_hbm.1, s32[24]{0:T(128)} %right_dims_hbm.1, s32[24]{0:T(128)} %bitcast.1, s32[24]{0:T(128)} %slot_hbm.1, bf16[1,8,256,256]{3,2,1,0:T(8,128)(2,1)} %left_hbm.1, bf16[24,4,256,256]{3,2,1,0:T(8,128)(2,1)} %psi_hbm.1, ...), custom_call_target="tpu_custom_call" | custom-call | tf_op jit(solution)/shard_map/pallas_call | solution.py:306
  78.3 1.1 %copy.10 = bf16[24,4,32,256]{3,2,1,0:T(8,128)(2,1)} copy(bf16[24,4,32,256]{3,2,1,0:T(8,128)(2,1)S(1)} %shard_map.82) | data formatting | bytes 3145728

commit v7 on v6

--- a/solution.py
+++ b/solution.py
@@ -16,7 +16,7 @@
 OWNERS = SIDE * SIDE
 CAP = 2
 PHASES = Z
-PSI_READ = 2
+PSI_READ = 4
 RIGHT_READ = 4
 ASKING = 7
 ALONE = 10
@@ -224,7 +224,7 @@
         part = (pl.ds(start, size), pl.ds(first, num))
         copy = pltpu.make_async_remote_copy(
             src_ref=give[p].at[part], dst_ref=got[p].at[part], send_sem=g_send.at[p],
-            recv_sem=g_recv.at[c, g], device_id=(partner, me), device_id_type=MESH,
+            recv_sem=g_recv.at[c % 2, g], device_id=(partner, me), device_id_type=MESH,
         )
         copy.start()
         return copy
@@ -334,7 +334,7 @@
             dma((blocks // RIGHT_READ,)),
             dma,
             dma((PHASES,)),
-            dma((chunks, MOST)),
+            dma((2, MOST)),
             dma((PHASES - 1,)),
             dma((chunks - 1, MOST)),
         ],

time: 79.5 us -> 79.4 us (level)
  no operation moved by 1% of the time
where the time goes in v7:
time: 79.4 us; the launch traced here: 79.3 us
  Pallas kernels  78.1 us (98%)
  local copies, waits for them, and re-layouts  1.15 us (1%)
    pallas_call x1, Pallas kernels, on_device(): pl.pallas_call(kernel, out_shape=pltpu.VMEM((blocks, states, rows, width)...  78.1 us

profile of v7, /device:TPU:0, one launch (start us, length us, event | category | flops | bytes accessed | tf_op | source)
XLA Modules:
  0.0 79.3 jit_solution(1671474989030238485)
XLA Ops:
  0.0 78.1 %shard_map.82 = bf16[24,4,32,256]{3,2,1,0:T(8,128)(2,1)S(1)} custom-call(f32[1,4,4]{2,1,0:T(4,128)} %mpo_hbm.1, s32[8]{0:T(128)} %left_dims_hbm.1, s32[24]{0:T(128)} %right_dims_hbm.1, s32[24]{0:T(128)} %bitcast.1, s32[24]{0:T(128)} %slot_hbm.1, bf16[1,8,256,256]{3,2,1,0:T(8,128)(2,1)} %left_hbm.1, bf16[24,4,256,256]{3,2,1,0:T(8,128)(2,1)} %psi_hbm.1, ...), custom_call_target="tpu_custom_call" | custom-call | tf_op jit(solution)/shard_map/pallas_call | solution.py:306
  78.2 1.1 %copy.10 = bf16[24,4,32,256]{3,2,1,0:T(8,128)(2,1)} copy(bf16[24,4,32,256]{3,2,1,0:T(8,128)(2,1)S(1)} %shard_map.82) | data formatting | bytes 3145728
